TPU v7x, 32 devices: a whole 2x2x4 slice. The times are simulated.
32 devices in a mesh: pos: 4 (over y, core), mom: 8 (over z, x).
Axes of the slice: x: 2, y: 2, z: 4, core: 2. Of those that a mesh axis runs over, the one named last changes fastest.
Arguments:
- quasi_probability_grid: float32 [2, 512, 8192], P(None, 'pos', 'mom'), may hold values from 0 to 2
- potential_energy_map: float32 [2, 512], P(None, 'pos'), may hold values from -3 to 3
- contact_inflow_states: float32 [2, 2, 8192], P(None, None, 'mom'), may hold values from 0 to 2
- crystal_kelvin_field: float32 [512], P('pos'), may hold values from 0.6 to 1.6
- area_index_map: int32 [512], P('pos'), may hold values from 0 to 3
- damping_ratio_per_step: float32 [4], replicated, may hold values from 0.05 to 0.5
- equilibrium_populace: float32 [4], replicated, may hold values from 0.5 to 2
- conductance_per_step: float32 [4], replicated, may hold values from 0.05 to 0.45
Outputs:
- wigner_updated: float32 [2, 512, 8192], P(None, 'pos', 'mom')
- phonon_warmth_updated: float32 [512], P('pos')
All inputs are finite; a program needn't handle non-finite values.
Results may differ from a plain program's by a relative error of at most 0.0003.
Values sent between devices are 32-bit elements; how exact they have to be, the bound alone decides.
A program may use at most 64 MiB of HBM per device.

v0:
```python
import functools

import jax
import jax.numpy as jnp
import numpy as np
from jax import lax
from jax.experimental import pallas as pl
from jax.experimental.pallas import tpu as pltpu
from jax.sharding import PartitionSpec as P

K = 8192
LANES = 128
FOLD = K // LANES
HALF = FOLD // 2

courant = 0.9
energy_top = 3.0
energy_shift = 0.25
band_offset = 0.5
potential_gain = 0.5
heat_gain = 0.5
heat_outflow = 0.1

F32 = jnp.float32
BF16 = jnp.bfloat16
MESH = pl.DeviceIdType.MESH


def unit_root(step, length):
    angle = 2.0 * np.pi * step / length
    return float(np.cos(angle)), float(np.sin(angle))


def turned(re, im, c, s):
    if s == 0.0 and c == 1.0:
        return re, im
    if im is None:
        return re * c, re * s
    if abs(c) < 1e-12:
        return -im * s, re * s
    return re * c - im * s, re * s + im * c


def plus(a, b):
    if a is None:
        return b
    if b is None:
        return a
    return a + b


def minus(a, b):
    if b is None:
        return a
    if a is None:
        return -b
    return a - b


def real_forward(xs):
    n = len(xs)
    if n == 2:
        return [(xs[0] + xs[1], None), (xs[0] - xs[1], None)]
    even, odd = real_forward(xs[0::2]), real_forward(xs[1::2])
    out = [None] * (n // 2 + 1)
    for k in range(n // 4 + 1):
        c, s = unit_root(k, n)
        orr, oi = turned(odd[k][0], odd[k][1], c, s)
        er, ei = even[k]
        if 4 * k == n:
            out[k] = (er, odd[k][0])
            continue
        out[k] = (er + orr, plus(ei, oi))
        low = minus(oi, ei)
        out[n // 2 - k] = (er - orr, low)
    return out


def real_inverse(spec):
    n = 2 * (len(spec) - 1)
    if n == 2:
        a, b = spec[0][0], spec[1][0]
        return [a + b, a - b]
    even, odd = [], []
    for k in range(n // 4 + 1):
        ar, ai = spec[k]
        br, bi = spec[n // 2 - k]
        c, s = unit_root(k, n)
        if 4 * k == n:
            even.append((ar + ar, None))
            odd.append((-(ai + ai), None))
            continue
        if k == 0:
            even.append((ar + br, None))
            odd.append((ar - br, None))
            continue
        even.append((ar + br, minus(ai, bi)))
        odd.append(turned(ar - br, plus(ai, bi), c, s))
    xe, xo = real_inverse(even), real_inverse(odd)
    out = [None] * n
    out[0::2], out[1::2] = xe, xo
    return out


def fill_tables(weight_ref, twist_ref):
    row = lax.broadcasted_iota(jnp.int32, (LANES, LANES), 0)
    lane = lax.broadcasted_iota(jnp.int32, (LANES, LANES), 1)
    angle = lax.rem(row * lane, LANES).astype(F32) * (2.0 * np.pi / LANES)
    c, s = jnp.cos(angle), jnp.sin(angle)
    for n, blocks in enumerate((((c, s), (-s, c)), ((c, -s), (s, c)))):
        for a in range(2):
            for b in range(2):
                at = (pl.ds(a * LANES, LANES), pl.ds(b * LANES, LANES))
                high = blocks[a][b].astype(BF16)
                weight_ref[(2 * n,) + at] = high
                weight_ref[(2 * n + 1,) + at] = (blocks[a][b] - high.astype(F32)).astype(BF16)
    count = twist_ref.shape[1]
    angle = (row * lane)[:count].astype(F32) * (2.0 * np.pi / K)
    twist_ref[0] = jnp.cos(angle)
    twist_ref[1] = jnp.sin(angle)


def split_dot(a, high, low):
    a_high = a.astype(BF16)
    a_low = (a - a_high.astype(F32)).astype(BF16)
    dot = functools.partial(jnp.dot, preferred_element_type=F32)
    return dot(a_high, high) + (dot(a_low, high) + dot(a_high, low))


def kernel(
    sizes,
    grid_hbm,
    pot_ref,
    contact_ref,
    warmth_ref,
    area_ref,
    damping_ref,
    populace_ref,
    conduct_ref,
    out_ref,
    warm_ref,
    grid_ref,
    weight_ref,
    twist_ref,
    recv,
    back_send,
    back_recv,
    halo_low,
    halo_high,
    pot_all,
    warmth_all,
    heat_send,
    heat_all,
    pot_table,
    work,
    fwd_send_sem,
    fwd_recv_sem,
    ret_send_sem,
    ret_recv_sem,
    halo_send_sem,
    halo_recv_sem,
    small_send_sem,
    small_recv_sem,
    heat_send_sem,
    heat_recv_sem,
    load_sem,
):
    bands, rows, cols, n_pos, n_mom = sizes
    share = rows // n_mom
    pieces = cols // LANES
    grid_len = n_pos * rows
    pos = lax.axis_index("pos")
    me = lax.axis_index("mom")

    def mom_peer(d):
        return lax.rem(me + d, n_mom)

    def pos_peer(d):
        return lax.rem(pos + d, n_pos)

    order = list(range(1, n_mom))
    loads = [
        pltpu.make_async_copy(grid_hbm, grid_ref, load_sem.at[0]),
    ]

    barrier = pltpu.get_barrier_semaphore()
    for d in range(1, n_mom):
        pl.semaphore_signal(barrier, inc=1, device_id=(pos, mom_peer(d)), device_id_type=MESH)
    for d in range(1, n_pos):
        pl.semaphore_signal(barrier, inc=1, device_id=(pos_peer(d), me), device_id_type=MESH)
    for load in loads:
        load.start()
    pl.semaphore_wait(barrier, n_mom - 1 + n_pos - 1)

    def small_copy(d, which):
        return pltpu.make_async_remote_copy(
            src_ref=warmth_ref if which else pot_ref,
            dst_ref=(warmth_all if which else pot_all).at[pos],
            send_sem=small_send_sem.at[which, d],
            recv_sem=small_recv_sem.at[which, d],
            device_id=(pos_peer(d), me),
            device_id_type=MESH,
        )

    def halo_copy(up):
        return pltpu.make_async_remote_copy(
            src_ref=grid_hbm.at[:, pl.ds(rows - 8, 8) if up else pl.ds(0, 8), :],
            dst_ref=halo_low if up else halo_high,
            send_sem=halo_send_sem.at[0 if up else 1],
            recv_sem=halo_recv_sem.at[0 if up else 1],
            device_id=(pos_peer(1 if up else n_pos - 1), me),
            device_id_type=MESH,
        )

    def forward_copy(band, d):
        peer = mom_peer(d)
        return pltpu.make_async_remote_copy(
            src_ref=grid_hbm.at[band, pl.ds(pl.multiple_of(peer * share, share), share), :],
            dst_ref=recv.at[band, me],
            send_sem=fwd_send_sem.at[band, d],
            recv_sem=fwd_recv_sem.at[band, d],
            device_id=(pos, peer),
            device_id_type=MESH,
        )

    def return_copy(band, d):
        peer = mom_peer(d)
        return pltpu.make_async_remote_copy(
            src_ref=back_send.at[band, peer],
            dst_ref=back_recv.at[band, me],
            send_sem=ret_send_sem.at[band, d],
            recv_sem=ret_recv_sem.at[band, d],
            device_id=(pos, peer),
            device_id_type=MESH,
        )

    def heat_copy(d):
        return pltpu.make_async_remote_copy(
            src_ref=heat_send,
            dst_ref=heat_all.at[me],
            send_sem=heat_send_sem.at[d],
            recv_sem=heat_recv_sem.at[d],
            device_id=(pos, mom_peer(d)),
            device_id_type=MESH,
        )

    for d in order:
        forward_copy(0, d).start()
    for d in range(1, n_pos):
        small_copy(d, 0).start()
        small_copy(d, 1).start()

    @pl.when(pos < n_pos - 1)
    def _():
        halo_copy(True).start()

    @pl.when(pos > 0)
    def _():
        halo_copy(False).start()

    for band in range(1, bands):
        for d in order:
            forward_copy(band, d).start()
    for load in loads:
        load.wait()
    fill_tables(weight_ref, twist_ref)

    own = pl.ds(pl.multiple_of(me * share, share), share)
    for band in range(bands):
        recv[band, me] = grid_ref[band, own, :]
    pot_all[pos] = pot_ref[...]
    warmth_all[pos] = warmth_ref[...]

    @pl.when(pos == 0)
    def _():
        halo_low[:, 7:8, :] = contact_ref[:, 0:1, :]

    @pl.when(pos > 0)
    def _():
        halo_copy(True).wait_recv()

    @pl.when(pos == n_pos - 1)
    def _():
        halo_high[:, 0:1, :] = contact_ref[:, 1:2, :]

    @pl.when(pos < n_pos - 1)
    def _():
        halo_copy(False).wait_recv()

    def picked(values):
        total = jnp.zeros((1, rows), F32)
        for n in range(values.shape[1]):
            total = jnp.where(area_ref[...] == n, values[0:1, n : n + 1], total)
        return total

    def column(row):
        return jnp.transpose(jnp.broadcast_to(row, (rows, rows)))

    warmth = warmth_ref[...]
    relax = picked(damping_ref)
    conduct = picked(conduct_ref)
    warmth_col = column(warmth)
    relax_col = column(relax)
    dens_col = column(picked(populace_ref))
    cold_col = -1.0 / warmth_col
    row_iota = lax.broadcasted_iota(jnp.int32, (rows, LANES), 0)

    def local_piece(c, heat):
        lane = pl.ds(pl.multiple_of(c * LANES, LANES), LANES)
        mom = lax.broadcasted_iota(jnp.int32, (1, LANES), 1) + (me * cols + c * LANES)
        unit = (2.0 * mom.astype(F32) + 1.0) / K - 1.0
        velocity = courant * unit
        energy = energy_top * (unit + energy_shift) ** 2
        for band in range(bands):
            f = grid_ref[band, :, lane]
            below = jnp.where(row_iota == 0, halo_low[band, 7:8, lane], pltpu.roll(f, 1, 0))
            above = jnp.where(
                row_iota == rows - 1, halo_high[band, 0:1, lane], pltpu.roll(f, rows - 1, 0)
            )
            drift = -velocity * jnp.where(velocity > 0, f - below, above - f)
            excess = f - dens_col * jnp.exp((energy + band_offset * band) * cold_col)
            out_ref[band, :, lane] = f + drift - relax_col * excess
            heat = heat + energy * excess
        return heat

    heat = lax.fori_loop(0, pieces, local_piece, jnp.zeros((rows, LANES), F32))
    heat_row = jnp.sum(jnp.transpose(heat), axis=0, keepdims=True)
    heat_send[...] = jnp.broadcast_to(heat_row, (8, rows))
    heat_all[me] = jnp.broadcast_to(heat_row, (8, rows))
    for d in range(1, n_mom):
        heat_copy(d).start()

    for d in range(1, n_pos):
        small_copy(d, 0).wait_recv()
        small_copy(d, 1).wait_recv()
    n_step = grid_len // FOLD
    base = pos * rows + me * share - HALF
    turn = lax.rem(2 * grid_len - base, grid_len)
    step_iota = lax.broadcasted_iota(jnp.int32, (n_step, grid_len), 0)
    place_iota = lax.broadcasted_iota(jnp.int32, (LANES, LANES), 0)
    lane_iota = lax.broadcasted_iota(jnp.int32, (LANES, LANES), 1)
    signed = jnp.where(lane_iota < LANES // 2, lane_iota, lane_iota - LANES) * FOLD
    for band in range(bands):
        profile = jnp.concatenate(
            [pot_all[j, band : band + 1, :] for j in range(n_pos)], axis=1
        )
        first = profile[:, 0:1]
        last = profile[:, grid_len - 1 : grid_len]
        profile = jnp.broadcast_to(profile, (n_step, grid_len))
        for side in range(2):
            stack = profile
            for m in range(1, n_step):
                shift = (grid_len - FOLD * m) % grid_len if side == 0 else FOLD * m
                stack = jnp.where(step_iota == m, pltpu.roll(profile, shift, 1), stack)
            stack = pltpu.roll(stack, turn, 1)[:, :LANES]
            stack = jnp.transpose(jnp.concatenate([stack] * (LANES // n_step), axis=0))
            index = base + place_iota + (signed if side == 0 else -signed)
            stack = jnp.where(index < 0, first, jnp.where(index > grid_len - 1, last, stack))
            pot_table[band, side] = stack

    scale = potential_gain / K

    def one_band(band, carry):
        for d in range(1, n_mom):
            forward_copy(band, d).wait_recv()
        cells = [
            recv[band, j, :, c * LANES : (c + 1) * LANES]
            for j in range(n_mom)
            for c in range(pieces)
        ]
        spec = real_forward(cells)
        for s, (re, im) in enumerate(spec):
            at = pl.ds(s * share, share)
            c_row, s_row = twist_ref[0, s : s + 1, :], twist_ref[1, s : s + 1, :]
            if im is None:
                work[at, :LANES] = re * c_row
                work[at, LANES:] = re * s_row
            else:
                work[at, :LANES] = re * c_row - im * s_row
                work[at, LANES:] = re * s_row + im * c_row
        work[...] = split_dot(work[...], weight_ref[0], weight_ref[1])
        for s in range(HALF + 1):
            at = pl.ds(s * share, share)
            differ = (
                pot_table[band, 0, HALF + s : HALF + s + share, :]
                - pot_table[band, 1, HALF - s : HALF - s + share, :]
            ) * scale
            work[at, :LANES] = work[at, :LANES] * differ
            work[at, LANES:] = work[at, LANES:] * differ
        work[...] = split_dot(work[...], weight_ref[2], weight_ref[3])
        spec = []
        for s in range(HALF + 1):
            at = pl.ds(s * share, share)
            c_row, s_row = twist_ref[0, s : s + 1, :], twist_ref[1, s : s + 1, :]
            re, im = work[at, :LANES], work[at, LANES:]
            spec.append((im * c_row - re * s_row, re * c_row + im * s_row))
        cells = real_inverse(spec)
        for j in range(n_mom):
            for c in range(pieces):
                back_send[band, j, :, c * LANES : (c + 1) * LANES] = cells[j * pieces + c]
        for d in order:
            return_copy(band, d).start()
        back_recv[band, me] = back_send[band, me]
        return carry

    lax.fori_loop(0, bands, one_band, 0)

    for d in range(1, n_mom):
        heat_copy(d).wait_recv()
    total = heat_all[0, 0:1, :]
    for j in range(1, n_mom):
        total = total + heat_all[j, 0:1, :]
    lane_row = lax.broadcasted_iota(jnp.int32, (1, rows), 1)
    low_edge = warmth_all[jnp.maximum(pos - 1, 0), 0:1, rows - 1 : rows]
    high_edge = warmth_all[jnp.minimum(pos + 1, n_pos - 1), 0:1, 0:1]
    low_edge = jnp.where(pos == 0, jnp.ones_like(low_edge), low_edge)
    high_edge = jnp.where(pos == n_pos - 1, jnp.ones_like(high_edge), high_edge)
    before = jnp.where(lane_row == 0, low_edge, pltpu.roll(warmth, 1, 1))
    after = jnp.where(lane_row == rows - 1, high_edge, pltpu.roll(warmth, rows - 1, 1))
    warm_ref[...] = (
        warmth
        + conduct * (after - 2.0 * warmth + before)
        + heat_gain / K * relax * total
        - heat_outflow * (warmth - 1.0)
    )

    def add_back(band, carry):
        for d in range(1, n_mom):
            return_copy(band, d).wait_recv()
        for j in range(n_mom):
            at = pl.ds(j * share, share)
            out_ref[band, at, :] = out_ref[band, at, :] + back_recv[band, j]
        return carry

    lax.fori_loop(0, bands, add_back, 0)

    for d in range(1, n_pos):
        small_copy(d, 0).wait_send()
        small_copy(d, 1).wait_send()

    @pl.when(pos < n_pos - 1)
    def _():
        halo_copy(True).wait_send()

    @pl.when(pos > 0)
    def _():
        halo_copy(False).wait_send()

    for d in range(1, n_mom):
        heat_copy(d).wait_send()
        for band in range(bands):
            forward_copy(band, d).wait_send()
            return_copy(band, d).wait_send()


def body(
    quasi_probability_grid,
    potential_energy_map,
    contact_inflow_states,
    crystal_kelvin_field,
    area_index_map,
    damping_ratio_per_step,
    equilibrium_populace,
    conductance_per_step,
):
    bands, rows, cols = quasi_probability_grid.shape
    n_pos = lax.axis_size("pos")
    n_mom = lax.axis_size("mom")
    share = rows // n_mom
    vmem = pl.BlockSpec(memory_space=pltpu.VMEM)
    hbm = pl.BlockSpec(memory_space=pltpu.HBM)
    dma = pltpu.SemaphoreType.DMA
    updated, warm = pl.pallas_call(
        functools.partial(kernel, (bands, rows, cols, n_pos, n_mom)),
        out_shape=(
            jax.ShapeDtypeStruct((bands, rows, cols), F32),
            jax.ShapeDtypeStruct((1, rows), F32),
        ),
        in_specs=[hbm] + [vmem] * 7,
        out_specs=(vmem, vmem),
        scratch_shapes=[
            pltpu.VMEM((bands, rows, cols), F32),
            pltpu.VMEM((4, 2 * LANES, 2 * LANES), BF16),
            pltpu.VMEM((2, HALF + 8, LANES), F32),
            pltpu.VMEM((bands, n_mom, share, cols), F32),
            pltpu.VMEM((bands, n_mom, share, cols), F32),
            pltpu.VMEM((bands, n_mom, share, cols), F32),
            pltpu.VMEM((bands, 8, cols), F32),
            pltpu.VMEM((bands, 8, cols), F32),
            pltpu.VMEM((n_pos, bands, rows), F32),
            pltpu.VMEM((n_pos, 1, rows), F32),
            pltpu.VMEM((8, rows), F32),
            pltpu.VMEM((n_mom, 8, rows), F32),
            pltpu.VMEM((bands, 2, LANES, LANES), F32),
            pltpu.VMEM(((HALF + 1) * share, 2 * LANES), F32),
            dma((bands, n_mom)),
            dma((bands, n_mom)),
            dma((bands, n_mom)),
            dma((bands, n_mom)),
            dma((2,)),
            dma((2,)),
            dma((2, n_pos)),
            dma((2, n_pos)),
            dma((n_mom,)),
            dma((n_mom,)),
            dma((1,)),
        ],
        compiler_params=pltpu.CompilerParams(
            collective_id=0, has_side_effects=True, vmem_limit_bytes=52 * 1024 * 1024
        ),
    )(
        quasi_probability_grid,
        potential_energy_map,
        contact_inflow_states,
        crystal_kelvin_field[None],
        area_index_map[None],
        damping_ratio_per_step[None],
        equilibrium_populace[None],
        conductance_per_step[None],
    )
    return updated, warm[0]


def solution(mesh):
    return jax.shard_map(
        body,
        mesh=mesh,
        in_specs=(
            P(None, "pos", "mom"),
            P(None, "pos"),
            P(None, None, "mom"),
            P("pos"),
            P("pos"),
            P(),
            P(),
            P(),
        ),
        out_specs=(P(None, "pos", "mom"), P("pos")),
        check_vma=False,
    )
```

profile of v0, /device:TPU:30, one launch (start us, length us, event | category | flops | bytes accessed | tf_op | source)
XLA Modules:
  0.0 54.7 jit_solution(10841288525254691730)
XLA Ops:
  0.6 0.0 copy-start.3
  0.6 0.0 copy-start.4
  0.7 0.0 copy-start.5
  0.7 0.0 copy-start.6
  0.7 0.0 copy-start.1
  0.7 0.0 copy-start.2
  0.7 0.6 %copy-done.3 = s32[128]{0:T(128)S(1)} copy-done((s32[128]{0:T(128)S(1)}, s32[128]{0:T(128)}, u32[]{:S(2)}) %copy-start.3) | copy-done | bytes 536
  1.3 0.0 copy-done.4
  1.3 0.0 copy-done.5
  1.3 0.0 copy-done.6
  1.3 0.0 copy-done.1
  1.4 0.0 copy-done.2
  1.4 0.0 copy-start
  1.4 0.7 %copy-done = f32[2,2,1024]{2,1,0:T(2,128)S(1)} copy-done((f32[2,2,1024]{2,1,0:T(2,128)S(1)}, f32[2,2,1024]{2,1,0:T(2,128)}, u32[]{:S(2)}) %copy-start) | copy-done | bytes 16408
  2.1 51.2 %shard_map.95 = (f32[2,128,1024]{2,1,0:T(8,128)S(1)}, f32[1,128]{1,0:T(1,128)S(1)}) custom-call(f32[2,128,1024]{2,1,0:T(8,128)} %grid_hbm.1, f32[2,128]{1,0:T(2,128)S(1)} %copy-done.1, f32[2,2,1024]{2,1,0:T(2,128)S(1)} %copy-done, f32[1,128]{1,0:T(1,128)S(1)} %bitcast.6, s32[1,128]{1,0:T(1,128)S(1)} %bitcast.7, f32[1,4]{1,0:T(1,128)S(1)} %bitcast.8, ...), custom_call_target="tpu_custom_call" | custom-call | tf_op jit(solution)/shard_map/pallas_call | solution.py:473
  53.3 1.0 %copy.12 = f32[2,128,1024]{2,1,0:T(8,128)} copy(f32[2,128,1024]{2,1,0:T(8,128)S(1)} %get-tuple-element.8) | data formatting | bytes 2097152
  54.2 0.5 copy.13
Async XLA Ops:
  0.6 0.7 %copy-start.3 = (s32[128]{0:T(128)S(1)}, s32[128]{0:T(128)}, u32[]{:S(2)}) copy-start(s32[128]{0:T(128)} %param.12) | copy-start | bytes 1540
  0.6 0.7 %copy-start.4 = (f32[4]{0:T(128)S(1)}, f32[4]{0:T(128)}, u32[]{:S(2)}) copy-start(f32[4]{0:T(128)} %param.13) | copy-start | bytes 52
  0.7 0.7 %copy-start.5 = (f32[4]{0:T(128)S(1)}, f32[4]{0:T(128)}, u32[]{:S(2)}) copy-start(f32[4]{0:T(128)} %param.14) | copy-start | bytes 52
  0.7 0.7 %copy-start.6 = (f32[4]{0:T(128)S(1)}, f32[4]{0:T(128)}, u32[]{:S(2)}) copy-start(f32[4]{0:T(128)} %param.15) | copy-start | bytes 52
  0.7 0.7 %copy-start.1 = (f32[2,128]{1,0:T(2,128)S(1)}, f32[2,128]{1,0:T(2,128)}, u32[]{:S(2)}) copy-start(f32[2,128]{1,0:T(2,128)} %pot_ref.1) | copy-start | bytes 3076
  0.7 0.7 %copy-start.2 = (f32[128]{0:T(128)S(1)}, f32[128]{0:T(128)}, u32[]{:S(2)}) copy-start(f32[128]{0:T(128)} %param.11) | copy-start | bytes 1540
  1.4 0.7 %copy-start = (f32[2,2,1024]{2,1,0:T(2,128)S(1)}, f32[2,2,1024]{2,1,0:T(2,128)}, u32[]{:S(2)}) copy-start(f32[2,2,1024]{2,1,0:T(2,128)} %contact_ref.1) | copy-start | bytes 49156
where the time goes:
time: 55.6 us; the launch traced here: 54.7 us
  Pallas kernels  51.2 us (92%)
  local copies, waits for them, and re-layouts  2.9 us (5%)
  between operations  0.69 us (1%)
    pallas_call x1, Pallas kernels, body(): pl.pallas_call(functools.partial(kernel, (bands, rows, cols, n_pos, n_mom...  51.2 us
    unnamed x16, local copies, waits for them, and re-layouts  2.9 us

commit v1 on v0

--- a/solution.py
+++ b/solution.py
@@ -130,6 +130,16 @@
 def kernel(
     sizes,
     grid_hbm,
+    pot_hbm,
+    contact_hbm,
+    warmth_hbm,
+    area_hbm,
+    damping_hbm,
+    populace_hbm,
+    conduct_hbm,
+    out_ref,
+    warm_ref,
+    grid_ref,
     pot_ref,
     contact_ref,
     warmth_ref,
@@ -137,9 +147,6 @@
     damping_ref,
     populace_ref,
     conduct_ref,
-    out_ref,
-    warm_ref,
-    grid_ref,
     weight_ref,
     twist_ref,
     recv,
@@ -161,9 +168,10 @@
     halo_recv_sem,
     small_send_sem,
     small_recv_sem,
-    heat_send_sem,
-    heat_recv_sem,
+    heat_sem,
     load_sem,
+    mom_ready,
+    pos_ready,
 ):
     bands, rows, cols, n_pos, n_mom = sizes
     share = rows // n_mom
@@ -172,32 +180,40 @@
     pos = lax.axis_index("pos")
     me = lax.axis_index("mom")
 
-    def mom_peer(d):
-        return lax.rem(me + d, n_mom)
+    level_size = inner_size(n_mom)
+    my_level, my_place = me // level_size, lax.rem(me, level_size)
 
     def pos_peer(d):
         return lax.rem(pos + d, n_pos)
 
-    order = list(range(1, n_mom))
+    def over_peers(do):
+        for d in range(1, n_mom):
+            do(lax.rem(me + d, n_mom))
+
+    def wait_all(ref, count, sem):
+        block = ref.at[pl.ds(0, count)]
+        pltpu.make_async_copy(block, block, sem).wait()
+
+    small = (
+        (pot_hbm, pot_ref),
+        (contact_hbm, contact_ref),
+        (warmth_hbm, warmth_ref),
+        (area_hbm, area_ref),
+        (damping_hbm, damping_ref),
+        (populace_hbm, populace_ref),
+        (conduct_hbm, conduct_ref),
+    )
     loads = [
-        pltpu.make_async_copy(grid_hbm, grid_ref, load_sem.at[0]),
+        pltpu.make_async_copy(src, dst, load_sem.at[n])
+        for n, (src, dst) in enumerate(((grid_hbm, grid_ref),) + small)
     ]
-
-    barrier = pltpu.get_barrier_semaphore()
-    for d in range(1, n_mom):
-        pl.semaphore_signal(barrier, inc=1, device_id=(pos, mom_peer(d)), device_id_type=MESH)
-    for d in range(1, n_pos):
-        pl.semaphore_signal(barrier, inc=1, device_id=(pos_peer(d), me), device_id_type=MESH)
-    for load in loads:
-        load.start()
-    pl.semaphore_wait(barrier, n_mom - 1 + n_pos - 1)
 
     def small_copy(d, which):
         return pltpu.make_async_remote_copy(
-            src_ref=warmth_ref if which else pot_ref,
+            src_ref=warmth_hbm if which else pot_hbm,
             dst_ref=(warmth_all if which else pot_all).at[pos],
-            send_sem=small_send_sem.at[which, d],
-            recv_sem=small_recv_sem.at[which, d],
+            send_sem=small_send_sem.at[which],
+            recv_sem=small_recv_sem.at[which],
             device_id=(pos_peer(d), me),
             device_id_type=MESH,
         )
@@ -212,40 +228,92 @@
             device_id_type=MESH,
         )
 
-    def forward_copy(band, d):
-        peer = mom_peer(d)
+    def forward_copy(band, peer):
         return pltpu.make_async_remote_copy(
             src_ref=grid_hbm.at[band, pl.ds(pl.multiple_of(peer * share, share), share), :],
             dst_ref=recv.at[band, me],
-            send_sem=fwd_send_sem.at[band, d],
-            recv_sem=fwd_recv_sem.at[band, d],
+            send_sem=fwd_send_sem.at[band],
+            recv_sem=fwd_recv_sem.at[band],
             device_id=(pos, peer),
             device_id_type=MESH,
         )
 
-    def return_copy(band, d):
-        peer = mom_peer(d)
+    def return_copy(band, peer):
         return pltpu.make_async_remote_copy(
             src_ref=back_send.at[band, peer],
             dst_ref=back_recv.at[band, me],
-            send_sem=ret_send_sem.at[band, d],
-            recv_sem=ret_recv_sem.at[band, d],
+            send_sem=ret_send_sem.at[band],
+            recv_sem=ret_recv_sem.at[band],
             device_id=(pos, peer),
             device_id_type=MESH,
         )
 
-    def heat_copy(d):
+    def heat_copy(peer):
         return pltpu.make_async_remote_copy(
             src_ref=heat_send,
             dst_ref=heat_all.at[me],
-            send_sem=heat_send_sem.at[d],
-            recv_sem=heat_recv_sem.at[d],
-            device_id=(pos, mom_peer(d)),
+            send_sem=heat_sem.at[0],
+            recv_sem=heat_sem.at[1],
+            device_id=(pos, peer),
             device_id_type=MESH,
         )
 
-    for d in order:
-        forward_copy(0, d).start()
+    def start_forward(band, peer):
+        forward_copy(band, peer).start()
+
+    for load in loads:
+        load.start()
+
+    barrier = pltpu.get_barrier_semaphore()
+    for peer in range(1, n_mom):
+
+        @pl.when(me < peer)
+        def _(peer=peer):
+            pl.semaphore_signal(barrier, inc=1, device_id=(pos, peer), device_id_type=MESH)
+
+    for peer in range(1, n_pos):
+
+        @pl.when(pos < peer)
+        def _(peer=peer):
+            pl.semaphore_signal(barrier, inc=1, device_id=(peer, me), device_id_type=MESH)
+
+    @pl.when(me + pos > 0)
+    def _():
+        pl.semaphore_wait(barrier, me + pos)
+
+    for peer in range(n_mom - 1):
+
+        @pl.when(peer < me)
+        def _(peer=peer):
+            pl.semaphore_signal(
+                mom_ready.at[my_level], inc=1, device_id=(pos, peer), device_id_type=MESH
+            )
+
+    for peer in range(n_pos - 1):
+
+        @pl.when(peer < pos)
+        def _(peer=peer):
+            pl.semaphore_signal(pos_ready, inc=1, device_id=(peer, me), device_id_type=MESH)
+
+    for peer in range(n_mom - 1):
+        pl.when(peer < me)(functools.partial(start_forward, 0, peer))
+
+    fill_tables(weight_ref, twist_ref)
+
+    for level in range(n_mom // level_size):
+        others = jnp.where(level == my_level, level_size - 1 - my_place, level_size)
+
+        @pl.when((level >= my_level) & (others > 0))
+        def _(level=level, others=others):
+            pl.semaphore_wait(mom_ready.at[level], others)
+
+        for peer in range(max(level * level_size, 1), (level + 1) * level_size):
+            pl.when(peer > me)(functools.partial(start_forward, 0, peer))
+
+    @pl.when(pos < n_pos - 1)
+    def _():
+        pl.semaphore_wait(pos_ready, n_pos - 1 - pos)
+
     for d in range(1, n_pos):
         small_copy(d, 0).start()
         small_copy(d, 1).start()
@@ -259,11 +327,9 @@
         halo_copy(False).start()
 
     for band in range(1, bands):
-        for d in order:
-            forward_copy(band, d).start()
+        over_peers(functools.partial(start_forward, band))
     for load in loads:
         load.wait()
-    fill_tables(weight_ref, twist_ref)
 
     own = pl.ds(pl.multiple_of(me * share, share), share)
     for band in range(bands):
@@ -327,12 +393,10 @@
     heat_row = jnp.sum(jnp.transpose(heat), axis=0, keepdims=True)
     heat_send[...] = jnp.broadcast_to(heat_row, (8, rows))
     heat_all[me] = jnp.broadcast_to(heat_row, (8, rows))
-    for d in range(1, n_mom):
-        heat_copy(d).start()
-
-    for d in range(1, n_pos):
-        small_copy(d, 0).wait_recv()
-        small_copy(d, 1).wait_recv()
+    over_peers(lambda peer: heat_copy(peer).start())
+
+    wait_all(pot_all, n_pos - 1, small_recv_sem.at[0])
+    wait_all(warmth_all, n_pos - 1, small_recv_sem.at[1])
     n_step = grid_len // FOLD
     base = pos * rows + me * share - HALF
     turn = lax.rem(2 * grid_len - base, grid_len)
@@ -360,9 +424,10 @@
 
     scale = potential_gain / K
 
-    def one_band(band, carry):
-        for d in range(1, n_mom):
-            forward_copy(band, d).wait_recv()
+    def forward_wait(band):
+        wait_all(recv.at[band], n_mom - 1, fwd_recv_sem.at[band])
+
+    def transform(band):
         cells = [
             recv[band, j, :, c * LANES : (c + 1) * LANES]
             for j in range(n_mom)
@@ -398,15 +463,30 @@
         for j in range(n_mom):
             for c in range(pieces):
                 back_send[band, j, :, c * LANES : (c + 1) * LANES] = cells[j * pieces + c]
-        for d in order:
-            return_copy(band, d).start()
         back_recv[band, me] = back_send[band, me]
+
+    def return_start(band):
+        over_peers(lambda peer: return_copy(band, peer).start())
+
+    def one_band(band, carry):
+        forward_wait(band)
+
+        transform(band)
+        return_start(band)
         return carry
 
     lax.fori_loop(0, bands, one_band, 0)
 
-    for d in range(1, n_mom):
-        heat_copy(d).wait_recv()
+    def add_back(band, carry):
+        wait_all(back_recv.at[band], n_mom - 1, ret_recv_sem.at[band])
+        for j in range(n_mom):
+            at = pl.ds(j * share, share)
+            out_ref[band, at, :] = out_ref[band, at, :] + back_recv[band, j]
+        return carry
+
+    lax.fori_loop(0, bands - 1, add_back, 0)
+
+    wait_all(heat_all, n_mom - 1, heat_sem.at[1])
     total = heat_all[0, 0:1, :]
     for j in range(1, n_mom):
         total = total + heat_all[j, 0:1, :]
@@ -424,19 +504,8 @@
         - heat_outflow * (warmth - 1.0)
     )
 
-    def add_back(band, carry):
-        for d in range(1, n_mom):
-            return_copy(band, d).wait_recv()
-        for j in range(n_mom):
-            at = pl.ds(j * share, share)
-            out_ref[band, at, :] = out_ref[band, at, :] + back_recv[band, j]
-        return carry
-
-    lax.fori_loop(0, bands, add_back, 0)
-
-    for d in range(1, n_pos):
-        small_copy(d, 0).wait_send()
-        small_copy(d, 1).wait_send()
+    wait_all(pot_all, n_pos - 1, small_send_sem.at[0])
+    wait_all(warmth_all, n_pos - 1, small_send_sem.at[1])
 
     @pl.when(pos < n_pos - 1)
     def _():
@@ -446,11 +515,33 @@
     def _():
         halo_copy(False).wait_send()
 
-    for d in range(1, n_mom):
-        heat_copy(d).wait_send()
-        for band in range(bands):
-            forward_copy(band, d).wait_send()
-            return_copy(band, d).wait_send()
+    wait_all(heat_all, n_mom - 1, heat_sem.at[0])
+    for band in range(bands):
+        wait_all(recv.at[band], n_mom - 1, fwd_send_sem.at[band])
+        if band < bands - 1:
+            wait_all(back_send.at[band], n_mom - 1, ret_send_sem.at[band])
+    add_back(bands - 1, 0)
+    wait_all(back_send.at[bands - 1], n_mom - 1, ret_send_sem.at[bands - 1])
+
+
+def write_out(grid_ref, warm_ref, grid_hbm, warm_hbm, sem):
+    bands = grid_ref.shape[0]
+    copies = [
+        pltpu.make_async_copy(grid_ref.at[band], grid_hbm.at[band], sem.at[band])
+        for band in range(bands)
+    ]
+    copies.append(pltpu.make_async_copy(warm_ref, warm_hbm, sem.at[bands]))
+    for copy in copies:
+        copy.start()
+    for copy in copies:
+        copy.wait()
+
+
+def inner_size(n):
+    inner = 1
+    while inner * inner * 4 <= n:
+        inner *= 2
+    return inner if n % inner == 0 else 1
 
 
 def body(
@@ -467,19 +558,29 @@
     n_pos = lax.axis_size("pos")
     n_mom = lax.axis_size("mom")
     share = rows // n_mom
+    kinds = damping_ratio_per_step.shape[0]
     vmem = pl.BlockSpec(memory_space=pltpu.VMEM)
     hbm = pl.BlockSpec(memory_space=pltpu.HBM)
     dma = pltpu.SemaphoreType.DMA
+    regular = pltpu.SemaphoreType.REGULAR
+    shapes = (
+        jax.ShapeDtypeStruct((bands, rows, cols), F32),
+        jax.ShapeDtypeStruct((1, rows), F32),
+    )
     updated, warm = pl.pallas_call(
         functools.partial(kernel, (bands, rows, cols, n_pos, n_mom)),
-        out_shape=(
-            jax.ShapeDtypeStruct((bands, rows, cols), F32),
-            jax.ShapeDtypeStruct((1, rows), F32),
-        ),
-        in_specs=[hbm] + [vmem] * 7,
+        out_shape=shapes,
+        in_specs=[hbm] * 8,
         out_specs=(vmem, vmem),
         scratch_shapes=[
             pltpu.VMEM((bands, rows, cols), F32),
+            pltpu.VMEM((bands, rows), F32),
+            pltpu.VMEM((bands, 2, cols), F32),
+            pltpu.VMEM((1, rows), F32),
+            pltpu.VMEM((1, rows), jnp.int32),
+            pltpu.VMEM((1, kinds), F32),
+            pltpu.VMEM((1, kinds), F32),
+            pltpu.VMEM((1, kinds), F32),
             pltpu.VMEM((4, 2 * LANES, 2 * LANES), BF16),
             pltpu.VMEM((2, HALF + 8, LANES), F32),
             pltpu.VMEM((bands, n_mom, share, cols), F32),
@@ -493,31 +594,45 @@
             pltpu.VMEM((n_mom, 8, rows), F32),
             pltpu.VMEM((bands, 2, LANES, LANES), F32),
             pltpu.VMEM(((HALF + 1) * share, 2 * LANES), F32),
-            dma((bands, n_mom)),
-            dma((bands, n_mom)),
-            dma((bands, n_mom)),
-            dma((bands, n_mom)),
+            dma((bands,)),
+            dma((bands,)),
+            dma((bands,)),
+            dma((bands,)),
             dma((2,)),
             dma((2,)),
-            dma((2, n_pos)),
-            dma((2, n_pos)),
-            dma((n_mom,)),
-            dma((n_mom,)),
-            dma((1,)),
+            dma((2,)),
+            dma((2,)),
+            dma((2,)),
+            dma((8,)),
+            regular((n_mom // inner_size(n_mom),)),
+            regular,
         ],
         compiler_params=pltpu.CompilerParams(
             collective_id=0, has_side_effects=True, vmem_limit_bytes=52 * 1024 * 1024
         ),
     )(
-        quasi_probability_grid,
-        potential_energy_map,
-        contact_inflow_states,
-        crystal_kelvin_field[None],
-        area_index_map[None],
-        damping_ratio_per_step[None],
-        equilibrium_populace[None],
-        conductance_per_step[None],
+        *(
+            pltpu.with_memory_space_constraint(operand, pltpu.HBM)
+            for operand in (
+                quasi_probability_grid,
+                potential_energy_map,
+                contact_inflow_states,
+                crystal_kelvin_field[None],
+                area_index_map[None],
+                damping_ratio_per_step[None],
+                equilibrium_populace[None],
+                conductance_per_step[None],
+            )
+        )
     )
+    updated, warm = pl.pallas_call(
+        write_out,
+        out_shape=shapes,
+        in_specs=[vmem, vmem],
+        out_specs=(hbm, hbm),
+        scratch_shapes=[dma((bands + 1,))],
+        compiler_params=pltpu.CompilerParams(vmem_limit_bytes=8 * 1024 * 1024),
+    )(updated, warm)
     return updated, warm[0]
 
 

time: 55.6 us -> 52.1 us (0.937); the launches traced: 54.7 us -> 52 us
  local copies, waits for them, and re-layouts: 2.9 us -> 0 us
    unnamed x16 -> x0, local copies, waits for them, and re-layouts: 2.9 us -> none
    pallas_call x0 -> x1, Pallas kernels: none -> 1 us  [body(): pl.pallas_call(write_out, out_shape=shapes, in_specs=[vmem, vmem], out_sp...]
    pallas_call x1, Pallas kernels: 51.2 us -> 50.3 us  [body(): pl.pallas_call(functools.partial(kernel, (bands, rows, cols, n_pos, n_mom...]
where the time goes in v1:
time: 52.1 us; the launch traced here: 52 us
  Pallas kernels  51.3 us (98%)
  between operations  0.64 us (1%)
    pallas_call x1, Pallas kernels, body(): pl.pallas_call(functools.partial(kernel, (bands, rows, cols, n_pos, n_mom...  50.3 us

profile of v1, /device:TPU:30, one launch (start us, length us, event | category | flops | bytes accessed | tf_op | source)
XLA Modules:
  0.0 52.0 jit_solution(891003975943031141)
XLA Ops:
  0.6 50.3 %shard_map.95 = (f32[2,128,1024]{2,1,0:T(8,128)S(1)}, f32[1,128]{1,0:T(1,128)S(1)}) custom-call(f32[2,128,1024]{2,1,0:T(8,128)} %grid_hbm.1, f32[2,128]{1,0:T(2,128)} %pot_hbm.1, f32[2,2,1024]{2,1,0:T(2,128)} %contact_hbm.1, f32[1,128]{1,0:T(1,128)} %bitcast.6, s32[1,128]{1,0:T(1,128)} %bitcast.7, f32[1,4]{1,0:T(1,128)} %bitcast.8, f32[1,4]{1,0:T(1,128)} %bitcast.9, ...), custom_call_target="tpu_custom_call" | custom-call | tf_op jit(solution)/shard_map/pallas_call | solution.py:570
  51.0 1.0 %shard_map.96 = (f32[2,128,1024]{2,1,0:T(8,128)}, f32[1,128]{1,0:T(1,128)}) custom-call(f32[2,128,1024]{2,1,0:T(8,128)S(1)} %get-tuple-element.6.grid_ref, f32[1,128]{1,0:T(1,128)S(1)} %get-tuple-element.7.warm_ref), custom_call_target="tpu_custom_call" | custom-call | tf_op jit(solution)/shard_map/pallas_call | solution.py:628

commit v2 on v1

--- a/solution.py
+++ b/solution.py
@@ -391,8 +391,8 @@
 
     heat = lax.fori_loop(0, pieces, local_piece, jnp.zeros((rows, LANES), F32))
     heat_row = jnp.sum(jnp.transpose(heat), axis=0, keepdims=True)
-    heat_send[...] = jnp.broadcast_to(heat_row, (8, rows))
-    heat_all[me] = jnp.broadcast_to(heat_row, (8, rows))
+    heat_send[...] = heat_row
+    heat_all[me] = heat_row
     over_peers(lambda peer: heat_copy(peer).start())
 
     wait_all(pot_all, n_pos - 1, small_recv_sem.at[0])
@@ -487,9 +487,9 @@
     lax.fori_loop(0, bands - 1, add_back, 0)
 
     wait_all(heat_all, n_mom - 1, heat_sem.at[1])
-    total = heat_all[0, 0:1, :]
+    total = heat_all[0]
     for j in range(1, n_mom):
-        total = total + heat_all[j, 0:1, :]
+        total = total + heat_all[j]
     lane_row = lax.broadcasted_iota(jnp.int32, (1, rows), 1)
     low_edge = warmth_all[jnp.maximum(pos - 1, 0), 0:1, rows - 1 : rows]
     high_edge = warmth_all[jnp.minimum(pos + 1, n_pos - 1), 0:1, 0:1]
@@ -590,8 +590,8 @@
             pltpu.VMEM((bands, 8, cols), F32),
             pltpu.VMEM((n_pos, bands, rows), F32),
             pltpu.VMEM((n_pos, 1, rows), F32),
-            pltpu.VMEM((8, rows), F32),
-            pltpu.VMEM((n_mom, 8, rows), F32),
+            pltpu.VMEM((1, rows), F32),
+            pltpu.VMEM((n_mom, 1, rows), F32),
             pltpu.VMEM((bands, 2, LANES, LANES), F32),
             pltpu.VMEM(((HALF + 1) * share, 2 * LANES), F32),
             dma((bands,)),

time: 52.1 us -> 51.5 us (0.988)
  Pallas kernels: 51.3 us -> 50.7 us
    pallas_call x1, Pallas kernels: 50.3 us -> 49.7 us  [body(): pl.pallas_call(functools.partial(kernel, (bands, rows, cols, n_pos, n_mom...]
where the time goes in v2:
time: 51.5 us; the launch traced here: 51.4 us
  Pallas kernels  50.7 us (98%)
  between operations  0.64 us (1%)
    pallas_call x1, Pallas kernels, body(): pl.pallas_call(functools.partial(kernel, (bands, rows, cols, n_pos, n_mom...  49.7 us

profile of v2, /device:TPU:30, one launch (start us, length us, event | category | flops | bytes accessed | tf_op | source)
XLA Modules:
  0.0 51.4 jit_solution(17879211707560288987)
XLA Ops:
  0.6 49.7 %shard_map.95 = (f32[2,128,1024]{2,1,0:T(8,128)S(1)}, f32[1,128]{1,0:T(1,128)S(1)}) custom-call(f32[2,128,1024]{2,1,0:T(8,128)} %grid_hbm.1, f32[2,128]{1,0:T(2,128)} %pot_hbm.1, f32[2,2,1024]{2,1,0:T(2,128)} %contact_hbm.1, f32[1,128]{1,0:T(1,128)} %bitcast.6, s32[1,128]{1,0:T(1,128)} %bitcast.7, f32[1,4]{1,0:T(1,128)} %bitcast.8, f32[1,4]{1,0:T(1,128)} %bitcast.9, ...), custom_call_target="tpu_custom_call" | custom-call | tf_op jit(solution)/shard_map/pallas_call | solution.py:570
  50.4 1.0 %shard_map.96 = (f32[2,128,1024]{2,1,0:T(8,128)}, f32[1,128]{1,0:T(1,128)}) custom-call(f32[2,128,1024]{2,1,0:T(8,128)S(1)} %get-tuple-element.6.grid_ref, f32[1,128]{1,0:T(1,128)S(1)} %get-tuple-element.7.warm_ref), custom_call_target="tpu_custom_call" | custom-call | tf_op jit(solution)/shard_map/pallas_call | solution.py:628

commit v3 on v2

--- a/solution.py
+++ b/solution.py
@@ -180,8 +180,9 @@
     pos = lax.axis_index("pos")
     me = lax.axis_index("mom")
 
-    level_size = inner_size(n_mom)
-    my_level, my_place = me // level_size, lax.rem(me, level_size)
+    mom_in = inner_size(n_mom)
+    mom_out = n_mom // mom_in
+    m_hi, m_lo = me // mom_in, lax.rem(me, mom_in)
 
     def pos_peer(d):
         return lax.rem(pos + d, n_pos)
@@ -265,29 +266,39 @@
         load.start()
 
     barrier = pltpu.get_barrier_semaphore()
-    for peer in range(1, n_mom):
-
-        @pl.when(me < peer)
-        def _(peer=peer):
-            pl.semaphore_signal(barrier, inc=1, device_id=(pos, peer), device_id_type=MESH)
-
     for peer in range(1, n_pos):
 
         @pl.when(pos < peer)
         def _(peer=peer):
             pl.semaphore_signal(barrier, inc=1, device_id=(peer, me), device_id_type=MESH)
 
-    @pl.when(me + pos > 0)
-    def _():
-        pl.semaphore_wait(barrier, me + pos)
-
-    for peer in range(n_mom - 1):
-
-        @pl.when(peer < me)
+    below = (m_hi + mom_out - 1) // mom_out + (m_lo + mom_in - 1) // mom_in + pos
+
+    @pl.when(below > 0)
+    def _():
+        pl.semaphore_wait(barrier, below)
+
+    @pl.when(m_hi < mom_out - 1)
+    def _():
+        pl.semaphore_signal(barrier, inc=1, device_id=(pos, me + mom_in), device_id_type=MESH)
+
+    @pl.when(m_lo < mom_in - 1)
+    def _():
+        pl.semaphore_signal(barrier, inc=1, device_id=(pos, me + 1), device_id_type=MESH)
+
+    def under(peer):
+        return (peer // mom_in <= m_hi) & (peer % mom_in <= m_lo) & (peer != me)
+
+    for peer in reversed(range(n_mom - 1)):
+
+        @pl.when(under(peer))
         def _(peer=peer):
             pl.semaphore_signal(
-                mom_ready.at[my_level], inc=1, device_id=(pos, peer), device_id_type=MESH
+                mom_ready.at[me], inc=1, device_id=(pos, peer), device_id_type=MESH
             )
+
+    for peer in range(n_mom - 1):
+        pl.when(under(peer))(functools.partial(start_forward, 0, peer))
 
     for peer in range(n_pos - 1):
 
@@ -295,20 +306,28 @@
         def _(peer=peer):
             pl.semaphore_signal(pos_ready, inc=1, device_id=(peer, me), device_id_type=MESH)
 
-    for peer in range(n_mom - 1):
-        pl.when(peer < me)(functools.partial(start_forward, 0, peer))
-
     fill_tables(weight_ref, twist_ref)
 
-    for level in range(n_mom // level_size):
-        others = jnp.where(level == my_level, level_size - 1 - my_place, level_size)
-
-        @pl.when((level >= my_level) & (others > 0))
-        def _(level=level, others=others):
-            pl.semaphore_wait(mom_ready.at[level], others)
-
-        for peer in range(max(level * level_size, 1), (level + 1) * level_size):
-            pl.when(peer > me)(functools.partial(start_forward, 0, peer))
+    steps = [(i, j) for i in range(mom_out) for j in range(mom_in) if i or j]
+    for d_hi, d_lo in sorted(steps, key=lambda step: (sum(step), -step[0])):
+        top_hi, top_lo = m_hi + d_hi, m_lo + d_lo
+        valid = (top_hi < mom_out) & (top_lo < mom_in)
+
+        @pl.when(valid)
+        def _(d_hi=d_hi, d_lo=d_lo, top_hi=top_hi, top_lo=top_lo):
+            pl.semaphore_wait(mom_ready.at[top_hi * mom_in + top_lo], 1)
+            if d_hi and d_lo:
+                start_forward(0, top_hi * mom_in + top_lo)
+            elif d_hi:
+                for lo in range(mom_in):
+                    pl.when(lo <= m_lo)(
+                        functools.partial(start_forward, 0, top_hi * mom_in + lo)
+                    )
+            else:
+                for hi in range(mom_out):
+                    pl.when(hi <= m_hi)(
+                        functools.partial(start_forward, 0, hi * mom_in + top_lo)
+                    )
 
     @pl.when(pos < n_pos - 1)
     def _():
@@ -604,7 +623,7 @@
             dma((2,)),
             dma((2,)),
             dma((8,)),
-            regular((n_mom // inner_size(n_mom),)),
+            regular((n_mom,)),
             regular,
         ],
         compiler_params=pltpu.CompilerParams(

time: 51.5 us -> 51.3 us (level)
  no operation moved by 1% of the time
where the time goes in v3:
time: 51.3 us; the launch traced here: 50.9 us
  Pallas kernels  50.3 us (98%)
  between operations  0.64 us (1%)
    pallas_call x1, Pallas kernels, body(): pl.pallas_call(functools.partial(kernel, (bands, rows, cols, n_pos, n_mom...  49.3 us

profile of v3, /device:TPU:30, one launch (start us, length us, event | category | flops | bytes accessed | tf_op | source)
XLA Modules:
  0.0 50.9 jit_solution(6313624236615592226)
XLA Ops:
  0.6 49.3 %shard_map.95 = (f32[2,128,1024]{2,1,0:T(8,128)S(1)}, f32[1,128]{1,0:T(1,128)S(1)}) custom-call(f32[2,128,1024]{2,1,0:T(8,128)} %grid_hbm.1, f32[2,128]{1,0:T(2,128)} %pot_hbm.1, f32[2,2,1024]{2,1,0:T(2,128)} %contact_hbm.1, f32[1,128]{1,0:T(1,128)} %bitcast.6, s32[1,128]{1,0:T(1,128)} %bitcast.7, f32[1,4]{1,0:T(1,128)} %bitcast.8, f32[1,4]{1,0:T(1,128)} %bitcast.9, ...), custom_call_target="tpu_custom_call" | custom-call | tf_op jit(solution)/shard_map/pallas_call | solution.py:589
  49.9 1.0 %shard_map.96 = (f32[2,128,1024]{2,1,0:T(8,128)}, f32[1,128]{1,0:T(1,128)}) custom-call(f32[2,128,1024]{2,1,0:T(8,128)S(1)} %get-tuple-element.6.grid_ref, f32[1,128]{1,0:T(1,128)S(1)} %get-tuple-element.7.warm_ref), custom_call_target="tpu_custom_call" | custom-call | tf_op jit(solution)/shard_map/pallas_call | solution.py:647

commit v4 on v3

--- a/solution.py
+++ b/solution.py
@@ -265,29 +265,41 @@
     for load in loads:
         load.start()
 
+    def under(peer):
+        return (peer // mom_in <= m_hi) & (peer % mom_in <= m_lo) & (peer != me)
+
+    def over(peer):
+        return (peer // mom_in >= m_hi) & (peer % mom_in >= m_lo) & (peer != me)
+
+    upper_row = mom_out // 2 if mom_out % 2 == 0 else mom_out
+    at_middle = m_hi == upper_row - 1 if mom_out % 2 == 0 else m_hi < 0
     barrier = pltpu.get_barrier_semaphore()
+
+    @pl.when(m_hi == upper_row)
+    def _():
+        pl.semaphore_signal(barrier, inc=1, device_id=(pos, me - mom_in), device_id_type=MESH)
+
+    for peer in range(1, n_mom):
+
+        @pl.when(over(peer))
+        def _(peer=peer):
+            pl.semaphore_signal(barrier, inc=1, device_id=(pos, peer), device_id_type=MESH)
+
     for peer in range(1, n_pos):
 
         @pl.when(pos < peer)
         def _(peer=peer):
             pl.semaphore_signal(barrier, inc=1, device_id=(peer, me), device_id_type=MESH)
 
-    below = (m_hi + mom_out - 1) // mom_out + (m_lo + mom_in - 1) // mom_in + pos
+    below = (m_hi + 1) * (m_lo + 1) - 1 + pos + jnp.where(at_middle, 1, 0)
 
     @pl.when(below > 0)
     def _():
         pl.semaphore_wait(barrier, below)
 
-    @pl.when(m_hi < mom_out - 1)
-    def _():
-        pl.semaphore_signal(barrier, inc=1, device_id=(pos, me + mom_in), device_id_type=MESH)
-
-    @pl.when(m_lo < mom_in - 1)
-    def _():
-        pl.semaphore_signal(barrier, inc=1, device_id=(pos, me + 1), device_id_type=MESH)
-
-    def under(peer):
-        return (peer // mom_in <= m_hi) & (peer % mom_in <= m_lo) & (peer != me)
+    @pl.when(at_middle)
+    def _():
+        start_forward(0, me + mom_in)
 
     for peer in reversed(range(n_mom - 1)):
 
@@ -320,7 +332,8 @@
                 start_forward(0, top_hi * mom_in + top_lo)
             elif d_hi:
                 for lo in range(mom_in):
-                    pl.when(lo <= m_lo)(
+                    done = at_middle & (lo == m_lo) if d_hi == 1 else lo < 0
+                    pl.when((lo <= m_lo) & jnp.logical_not(done))(
                         functools.partial(start_forward, 0, top_hi * mom_in + lo)
                     )
             else:

time: 51.3 us -> 50.7 us (0.988)
  Pallas kernels: 50.3 us -> 49.6 us
    pallas_call x1, Pallas kernels: 49.3 us -> 48.6 us  [body(): pl.pallas_call(functools.partial(kernel, (bands, rows, cols, n_pos, n_mom...]
where the time goes in v4:
time: 50.7 us; the launch traced here: 50.2 us
  Pallas kernels  49.6 us (98%)
  between operations  0.64 us (1%)
    pallas_call x1, Pallas kernels, body(): pl.pallas_call(functools.partial(kernel, (bands, rows, cols, n_pos, n_mom...  48.6 us

profile of v4, /device:TPU:30, one launch (start us, length us, event | category | flops | bytes accessed | tf_op | source)
XLA Modules:
  0.0 50.2 jit_solution(13884421673616547513)
XLA Ops:
  0.6 48.6 %shard_map.95 = (f32[2,128,1024]{2,1,0:T(8,128)S(1)}, f32[1,128]{1,0:T(1,128)S(1)}) custom-call(f32[2,128,1024]{2,1,0:T(8,128)} %grid_hbm.1, f32[2,128]{1,0:T(2,128)} %pot_hbm.1, f32[2,2,1024]{2,1,0:T(2,128)} %contact_hbm.1, f32[1,128]{1,0:T(1,128)} %bitcast.6, s32[1,128]{1,0:T(1,128)} %bitcast.7, f32[1,4]{1,0:T(1,128)} %bitcast.8, f32[1,4]{1,0:T(1,128)} %bitcast.9, ...), custom_call_target="tpu_custom_call" | custom-call | tf_op jit(solution)/shard_map/pallas_call | solution.py:602
  49.2 1.0 %shard_map.96 = (f32[2,128,1024]{2,1,0:T(8,128)}, f32[1,128]{1,0:T(1,128)}) custom-call(f32[2,128,1024]{2,1,0:T(8,128)S(1)} %get-tuple-element.6.grid_ref, f32[1,128]{1,0:T(1,128)S(1)} %get-tuple-element.7.warm_ref), custom_call_target="tpu_custom_call" | custom-call | tf_op jit(solution)/shard_map/pallas_call | solution.py:660

commit v5 on v4

--- a/solution.py
+++ b/solution.py
@@ -160,9 +160,8 @@
     heat_all,
     pot_table,
     work,
-    fwd_send_sem,
+    send_sem,
     fwd_recv_sem,
-    ret_send_sem,
     ret_recv_sem,
     halo_send_sem,
     halo_recv_sem,
@@ -233,7 +232,7 @@
         return pltpu.make_async_remote_copy(
             src_ref=grid_hbm.at[band, pl.ds(pl.multiple_of(peer * share, share), share), :],
             dst_ref=recv.at[band, me],
-            send_sem=fwd_send_sem.at[band],
+            send_sem=send_sem.at[0],
             recv_sem=fwd_recv_sem.at[band],
             device_id=(pos, peer),
             device_id_type=MESH,
@@ -243,7 +242,7 @@
         return pltpu.make_async_remote_copy(
             src_ref=back_send.at[band, peer],
             dst_ref=back_recv.at[band, me],
-            send_sem=ret_send_sem.at[band],
+            send_sem=send_sem.at[1],
             recv_sem=ret_recv_sem.at[band],
             device_id=(pos, peer),
             device_id_type=MESH,
@@ -301,6 +300,9 @@
     def _():
         start_forward(0, me + mom_in)
 
+    for peer in range(n_mom - 1):
+        pl.when(under(peer))(functools.partial(start_forward, 0, peer))
+
     for peer in reversed(range(n_mom - 1)):
 
         @pl.when(under(peer))
@@ -309,8 +311,6 @@
                 mom_ready.at[me], inc=1, device_id=(pos, peer), device_id_type=MESH
             )
 
-    for peer in range(n_mom - 1):
-        pl.when(under(peer))(functools.partial(start_forward, 0, peer))
 
     for peer in range(n_pos - 1):
 
@@ -548,12 +548,11 @@
         halo_copy(False).wait_send()
 
     wait_all(heat_all, n_mom - 1, heat_sem.at[0])
-    for band in range(bands):
-        wait_all(recv.at[band], n_mom - 1, fwd_send_sem.at[band])
-        if band < bands - 1:
-            wait_all(back_send.at[band], n_mom - 1, ret_send_sem.at[band])
+    sent = recv.at[:, pl.ds(0, n_mom - 1)]
+    pltpu.make_async_copy(sent, sent, send_sem.at[0]).wait()
     add_back(bands - 1, 0)
-    wait_all(back_send.at[bands - 1], n_mom - 1, ret_send_sem.at[bands - 1])
+    sent = back_send.at[:, pl.ds(0, n_mom - 1)]
+    pltpu.make_async_copy(sent, sent, send_sem.at[1]).wait()
 
 
 def write_out(grid_ref, warm_ref, grid_hbm, warm_hbm, sem):
@@ -626,8 +625,7 @@
             pltpu.VMEM((n_mom, 1, rows), F32),
             pltpu.VMEM((bands, 2, LANES, LANES), F32),
             pltpu.VMEM(((HALF + 1) * share, 2 * LANES), F32),
-            dma((bands,)),
-            dma((bands,)),
+            dma((2,)),
             dma((bands,)),
             dma((bands,)),
             dma((2,)),

time: 50.7 us -> 50.7 us (level)
  no operation moved by 1% of the time
where the time goes in v5:
time: 50.7 us; the launch traced here: 50.2 us
  Pallas kernels  49.6 us (98%)
  between operations  0.64 us (1%)
    pallas_call x1, Pallas kernels, body(): pl.pallas_call(functools.partial(kernel, (bands, rows, cols, n_pos, n_mom...  48.6 us

profile of v5, /device:TPU:30, one launch (start us, length us, event | category | flops | bytes accessed | tf_op | source)
XLA Modules:
  0.0 50.2 jit_solution(7173501623053845667)
XLA Ops:
  0.6 48.6 %shard_map.95 = (f32[2,128,1024]{2,1,0:T(8,128)S(1)}, f32[1,128]{1,0:T(1,128)S(1)}) custom-call(f32[2,128,1024]{2,1,0:T(8,128)} %grid_hbm.1, f32[2,128]{1,0:T(2,128)} %pot_hbm.1, f32[2,2,1024]{2,1,0:T(2,128)} %contact_hbm.1, f32[1,128]{1,0:T(1,128)} %bitcast.6, s32[1,128]{1,0:T(1,128)} %bitcast.7, f32[1,4]{1,0:T(1,128)} %bitcast.8, f32[1,4]{1,0:T(1,128)} %bitcast.9, ...), custom_call_target="tpu_custom_call" | custom-call | tf_op jit(solution)/shard_map/pallas_call | solution.py:601
  49.2 1.0 %shard_map.96 = (f32[2,128,1024]{2,1,0:T(8,128)}, f32[1,128]{1,0:T(1,128)}) custom-call(f32[2,128,1024]{2,1,0:T(8,128)S(1)} %get-tuple-element.6.grid_ref, f32[1,128]{1,0:T(1,128)S(1)} %get-tuple-element.7.warm_ref), custom_call_target="tpu_custom_call" | custom-call | tf_op jit(solution)/shard_map/pallas_call | solution.py:658
